TPU v7x, 256 devices: a whole 4x4x8 slice. The times are simulated.
256 devices in a mesh: dp: 64 (over z, y, core), tensor: 4 (over x).
Axes of the slice: x: 4, y: 4, z: 8, core: 2. Of those that a mesh axis runs over, the one named last changes fastest.
Arguments:
- queries: bfloat16 [32768, 2048], P('dp', 'tensor'), may hold values from -360 to 360
- neighbours: int32 [512, 2], P('dp'), may hold values from 0 to 63, as said below
- counts: int32 [512], P('dp'), may hold values from 1 to 2
- states: bfloat16 [64, 128, 4096], P('dp'), may hold values from -6 to 6
- w_key: bfloat16 [4096, 2048], P('dp', 'tensor'), may hold values from -0.09375 to 0.09375
- w_value: bfloat16 [4096, 2048], P('dp', 'tensor'), may hold values from -0.09375 to 0.09375
- cotangent: bfloat16 [32768, 2048], P('dp', 'tensor'), may hold values from -6 to 6
Outputs:
- context: bfloat16 [32768, 2048], P('dp', 'tensor')
- query_grad: bfloat16 [32768, 2048], P('dp', 'tensor')
- state_grad: bfloat16 [64, 128, 4096], P('dp', None, 'tensor')
Inputs may be any that keep to these rules, and one draw needn't show every extreme that they name: Neighbour n is held by dp index n. Among the 16 slots of one index of dp, at most 1 name neighbours of one holder, and some holder is named exactly 1 times.
All inputs are finite; a program needn't handle non-finite values.
Results may differ from a plain program's by a relative error of at most 0.035.
The roundings to bfloat16 on the way count: a program that leaves them out, or rounds other values in their place, can miss the bound.
Values may be sent and summed in bfloat16 or wider, within the bound.
A program may use at most 128 MiB of HBM per device.

v0:
```python
import math
import jax
import jax.numpy as jnp
from jax import lax
from jax.sharding import PartitionSpec as P

HEAD = 128


def local(queries, neighbours, counts, states, w_key, w_value, cotangent):
    dp_count = lax.axis_size("dp")
    spans, neigh = neighbours.shape
    slots = spans * neigh
    capacity = (slots + dp_count - 1) // dp_count
    buffer_rows = dp_count * capacity
    nbr_dev, nbr_len, dmodel = states.shape
    local_width = queries.shape[1]
    heads_here = local_width // HEAD
    span_len = queries.shape[0] // spans
    score_scale = 1.0 / math.sqrt(HEAD)
    slot_ids = neighbours.reshape(slots)
    holder = slot_ids // nbr_dev
    slot_order = jnp.arange(slots, dtype=jnp.int32)
    earlier = (holder[:, None] == holder[None, :]) & (slot_order[None, :] < slot_order[:, None])
    holder_rank = jnp.sum(earlier.astype(jnp.int32), axis=1)
    position = holder * capacity + holder_rank
    placing = position[None, :] == jnp.arange(buffer_rows, dtype=jnp.int32)[:, None]
    place_half = placing.astype(jnp.bfloat16)
    place_full = placing.astype(jnp.float32)
    query_spans = queries.reshape(spans, 1, span_len * local_width)
    query_slots = jnp.broadcast_to(query_spans, (spans, neigh, span_len * local_width)).reshape(
        slots, span_len * local_width
    )
    send_query = jnp.dot(place_half, query_slots, preferred_element_type=jnp.float32).astype(
        jnp.bfloat16
    )
    send_query = send_query.reshape(dp_count, capacity, span_len, local_width)
    flat_states = states.reshape(nbr_dev * nbr_len, dmodel)
    key_full = lax.all_gather(w_key, "dp", axis=0, tiled=True)
    value_full = lax.all_gather(w_value, "dp", axis=0, tiled=True)
    key_acc = jnp.dot(flat_states, key_full, preferred_element_type=jnp.float32)
    value_acc = jnp.dot(flat_states, value_full, preferred_element_type=jnp.float32)
    key_rows = key_acc.astype(jnp.bfloat16).reshape(nbr_len, heads_here, HEAD)
    value_rows = value_acc.astype(jnp.bfloat16).reshape(nbr_len, heads_here, HEAD)
    key_rows, value_rows, key_full, value_full = (key_rows, value_rows, key_full, value_full)
    recv_query = lax.all_to_all(send_query, "dp", split_axis=0, concat_axis=0, tiled=True)
    lead = recv_query.shape[:-1]
    item_query = recv_query.reshape(lead + (heads_here, HEAD))
    scores = (
        jnp.einsum("abqhd,khd->abqhk", item_query, key_rows, preferred_element_type=jnp.float32)
        * score_scale
    )
    row_max = jnp.max(scores, axis=-1, keepdims=True)
    log_total = row_max[..., 0] + jnp.log(jnp.sum(jnp.exp(scores - row_max), axis=-1))
    prob_out = jnp.exp(scores - log_total[..., None])
    part_out = jnp.einsum(
        "abqhk,khd->abqhd",
        prob_out.astype(jnp.bfloat16),
        value_rows,
        preferred_element_type=jnp.float32,
    ).astype(jnp.bfloat16)
    item_part = part_out.reshape(lead + (local_width,))
    item_query = recv_query.reshape(dp_count, capacity, span_len, heads_here, HEAD)
    prob_half = prob_out.astype(jnp.bfloat16)
    back_part, back_log = (
        lax.all_to_all(
            item_part.astype(jnp.float32), "dp", split_axis=0, concat_axis=0, tiled=True
        ).astype(item_part.dtype),
        lax.all_to_all(log_total, "dp", split_axis=0, concat_axis=0, tiled=True),
    )
    back_part = back_part.reshape(buffer_rows, span_len, local_width)
    back_log = back_log.reshape(buffer_rows, span_len, heads_here)
    got_part = back_part[position].reshape(spans, neigh, span_len, heads_here, HEAD)
    got_log = back_log[position].reshape(spans, neigh, span_len, heads_here)
    is_valid = jnp.arange(neigh, dtype=jnp.int32)[None, :] < counts[:, None]
    live = is_valid[:, :, None, None]
    masked = jnp.where(live, got_log, -1e30)
    top_part = jnp.max(masked, axis=1, keepdims=True)
    raw_weight = jnp.where(live, jnp.exp(masked - top_part), 0.0)
    mix_weight = raw_weight / jnp.sum(raw_weight, axis=1, keepdims=True)
    part_full = got_part.astype(jnp.float32)
    mixed_rows = jnp.sum(mix_weight[..., None] * part_full, axis=1)
    context = mixed_rows.astype(jnp.bfloat16).reshape(spans * span_len, local_width)
    grad_rows = cotangent.astype(jnp.float32).reshape(spans, span_len, heads_here, HEAD)
    part_grad = lax.optimization_barrier(
        (mix_weight[..., None] * grad_rows[:, None]).astype(jnp.bfloat16)
    )
    lse_grad = mix_weight * jnp.sum(grad_rows[:, None] * (part_full - mixed_rows[:, None]), axis=-1)
    rest_term = jnp.sum(part_grad.astype(jnp.float32) * part_full, axis=-1) - lse_grad
    send_grad = jnp.dot(
        place_half,
        part_grad.reshape(slots, span_len * local_width),
        preferred_element_type=jnp.float32,
    ).astype(jnp.bfloat16)
    send_grad = send_grad.reshape(dp_count, capacity, span_len, local_width)
    send_rest = jnp.dot(
        place_full, rest_term.reshape(slots, span_len * heads_here), precision=lax.Precision.HIGHEST
    )
    send_rest = send_rest.reshape(dp_count, capacity, span_len, heads_here)
    recv_grad, recv_rest = (
        lax.all_to_all(
            send_grad.astype(jnp.float32), "dp", split_axis=0, concat_axis=0, tiled=True
        ).astype(send_grad.dtype),
        lax.all_to_all(send_rest, "dp", split_axis=0, concat_axis=0, tiled=True),
    )
    item_grad = recv_grad.reshape(dp_count, capacity, span_len, heads_here, HEAD)
    dprob = jnp.einsum(
        "abqhd,khd->abqhk", item_grad, value_rows, preferred_element_type=jnp.float32
    )
    dscore = prob_out * (dprob - recv_rest[..., None])
    dscore_half = dscore.astype(jnp.bfloat16)
    item_dq = (
        jnp.einsum("abqhk,khd->abqhd", dscore_half, key_rows, preferred_element_type=jnp.float32)
        * score_scale
    )
    item_dq = item_dq.astype(jnp.bfloat16).reshape(dp_count, capacity, span_len, local_width)
    back_dq = lax.all_to_all(item_dq, "dp", split_axis=0, concat_axis=0, tiled=True)
    key_grad = (
        jnp.einsum("abqhk,abqhd->khd", dscore_half, item_query, preferred_element_type=jnp.float32)
        * score_scale
    )
    key_grad = key_grad.astype(jnp.bfloat16).reshape(nbr_dev * nbr_len, local_width)
    value_grad = jnp.einsum(
        "abqhk,abqhd->khd", prob_half, item_grad, preferred_element_type=jnp.float32
    )
    value_grad = value_grad.astype(jnp.bfloat16).reshape(nbr_dev * nbr_len, local_width)
    contract = (((1,), (1,)), ((), ()))
    state_term = lax.dot_general(key_grad, key_full, contract, preferred_element_type=jnp.float32)
    state_term = state_term + lax.dot_general(
        value_grad, value_full, contract, preferred_element_type=jnp.float32
    )
    summed = lax.psum_scatter(
        state_term.astype(jnp.bfloat16), "tensor", scatter_dimension=1, tiled=True
    ).astype(jnp.float32)
    state_grad = summed.astype(jnp.bfloat16).reshape(nbr_dev, nbr_len, summed.shape[1])
    got_dq = back_dq.reshape(buffer_rows, span_len * local_width)[position]
    got_dq = got_dq.reshape(spans, neigh, span_len * local_width).astype(jnp.float32)
    query_grad = jnp.sum(got_dq, axis=1).astype(jnp.bfloat16).reshape(spans * span_len, local_width)
    return (context, query_grad, state_grad)


def solution(mesh):
    placed = (
        P("dp", "tensor"),
        P("dp", None),
        P("dp"),
        P("dp", None, None),
        P("dp", "tensor"),
        P("dp", "tensor"),
        P("dp", "tensor"),
    )
    return jax.shard_map(
        local,
        mesh=mesh,
        in_specs=placed,
        out_specs=(P("dp", "tensor"), P("dp", "tensor"), P("dp", None, "tensor")),
        check_vma=False,
    )
```

profile of v0, /device:TPU:4, one launch (start us, length us, event | category | flops | bytes accessed | tf_op | source)
XLA Modules:
  0.0 683.3 jit_solution(17984772549266577789)
XLA Ops:
  12.6 3.6 copy.107
  16.2 12.4 %all-to-all-start = ((bf16[64,1,64,512]{3,2,1,0:T(8,128)(2,1)}), bf16[64,1,64,512]{3,2,1,0:T(8,128)(2,1)}, u32[]{:S(2)}, u32[]{:S(2)}) async-start(bf16[64,1,64,512]{3,2,1,0:T(8,128)(2,1)} %bitcast.204), calls=%async_computation | async-start | bytes 8388608 | tf_op jit(solution)/shard_map/all_to_all | solution.py:46
  29.3 106.6 %all-to-all-done = bf16[64,1,64,512]{3,2,1,0:T(8,128)(2,1)} async-done(((bf16[64,1,64,512]{3,2,1,0:T(8,128)(2,1)}), bf16[64,1,64,512]{3,2,1,0:T(8,128)(2,1)}, u32[]{:S(2)}, u32[]{:S(2)}) %all-to-all-start) | async-done | bytes 4194336 | tf_op jit(solution)/shard_map/all_to_all | solution.py:46
  135.9 6.9 %reshape.264 = bf16[64,64,4,128]{3,2,1,0:T(4,128)(2,1)} reshape(bf16[64,1,64,512]{3,2,1,0:T(8,128)(2,1)} %all-to-all-done) | data formatting | bytes 8388608 | tf_op jit(solution)/shard_map/reshape
  142.8 5.3 copy.81
  156.1 4.8 fusion.2
  161.7 6.9 %all-to-all-start.1 = ((f32[64,1,256]{2,1,0:T(1,128)}), f32[64,1,256]{2,1,0:T(1,128)S(1)}, u32[]{:S(2)}, u32[]{:S(2)}) async-start(f32[64,1,256]{2,1,0:T(1,128)} %reshape.325), calls=%async_computation.1 | async-start | bytes 131072 | tf_op jit(solution)/shard_map/all_to_all | solution.py:69
  168.7 6.9 %fusion.4 = bf16[64,1,64,4,128]{4,2,0,3,1:T(8,128)(2,1)} fusion(f32[64,64,4]{1,0,2:T(8,128)S(1)} %log_add_fusion, f32[4,128,4096]{1,2,0} %copy-done.2), kind=kLoop, calls=%fused_computation.15 | loop fusion | flops 6291456 | bytes 12648448 | tf_op jit(solution)/shard_map/convert_element_type | solution.py:58
  175.6 19.9 %all-gather.5.cloned.1.call-done = bf16[4096,512]{1,0:T(8,128)(2,1)} async-done(((bf16[64,512]{1,0:T(8,128)(2,1)}), bf16[4096,512]{1,0:T(8,128)(2,1)}) %all-gather.5.cloned.1.call-update) | async-done | bytes 4194320 | tf_op jit(solution)/shard_map/all_gather | solution.py:40
  200.1 4.1 convert_bitcast_fusion
  204.2 14.6 %copy.86 = f32[64,1,64,4,128]{4,3,1,2,0:T(4,128)} copy(f32[64,1,64,4,128]{4,2,0,3,1:T(8,128)} %convert_bitcast_fusion) | data formatting | bytes 16777216 | tf_op jit(solution)/shard_map/convert_element_type | solution.py:67
  218.7 8.1 %convert_bitcast_fusion.1 = bf16[64,64,1,512]{3,2,1,0:T(2,128)(2,1)} fusion(f32[64,1,64,512]{3,1,2,0:T(1,128)} %bitcast.197), kind=kLoop, calls=%fused_computation.76 | loop fusion | flops 2097152 | bytes 12582912
  227.4 28.4 %reduce.4 = bf16[64,64,512]{2,1,0:T(8,128)(2,1)} reduce(bf16[64,64,1,512]{3,2,1,0:T(2,128)(2,1)} %convert_bitcast_fusion.1, bf16[]{:T(256)} %broadcast.138), dimensions={2}, to_apply=%convert_bitcast_fusion.1.reduce_sub_computation | reduce | bytes 8388610
  255.7 7.8 %reshape.323 = bf16[64,2,16384]{2,1,0:T(2,128)(2,1)} reshape(bf16[64,64,512]{2,1,0:T(8,128)(2,1)} %reduce.4) | data formatting | bytes 8388608
  263.6 7.6 %all-to-all-start.2 = ((bf16[64,2,16384]{2,1,0:T(2,128)(2,1)}), bf16[64,2,16384]{2,1,0:T(2,128)(2,1)}, u32[]{:S(2)}, u32[]{:S(2)}) async-start(bf16[64,2,16384]{2,1,0:T(2,128)(2,1)} %reshape.323), calls=%async_computation.2 | async-start | bytes 8388608 | tf_op jit(solution)/shard_map/all_to_all | solution.py:66
  279.0 88.4 %all-to-all-done.2 = bf16[64,2,16384]{2,1,0:T(2,128)(2,1)} async-done(((bf16[64,2,16384]{2,1,0:T(2,128)(2,1)}), bf16[64,2,16384]{2,1,0:T(2,128)(2,1)}, u32[]{:S(2)}, u32[]{:S(2)}) %all-to-all-start.2) | async-done | bytes 4194336 | tf_op jit(solution)/shard_map/all_to_all | solution.py:66
  367.4 19.7 %reshape.324 = bf16[64,64,1,512]{3,2,1,0:T(2,128)(2,1)} reshape(bf16[64,2,16384]{2,1,0:T(2,128)(2,1)} %all-to-all-done.2) | data formatting | bytes 8388608
  387.1 6.9 %copy.138 = bf16[64,1,64,512]{3,2,1,0:T(8,128)(2,1)} copy(bf16[64,1,64,512]{3,1,2,0:T(2,128)(2,1)} %bitcast.196) | data formatting | bytes 8388608
  397.6 5.2 multiply_convert_fusion.2
  405.4 4.8 multiply_reduce_fusion
  415.6 5.5 all-to-all-start.4
  423.7 3.6 copy.109
  427.3 3.8 all-to-all-done.4
  431.1 6.9 %all-to-all-start.3 = ((bf16[64,1,64,512]{3,2,1,0:T(8,128)(2,1)}), bf16[64,1,64,512]{3,2,1,0:T(8,128)(2,1)}, u32[]{:S(2)}, u32[]{:S(2)}) async-start(bf16[64,1,64,512]{3,2,1,0:T(8,128)(2,1)} %bitcast.203), calls=%async_computation.3 | async-start | bytes 8388608 | tf_op jit(solution)/shard_map/all_to_all | solution.py:101
  438.9 95.3 %all-to-all-done.3 = bf16[64,1,64,512]{3,2,1,0:T(8,128)(2,1)} async-done(((bf16[64,1,64,512]{3,2,1,0:T(8,128)(2,1)}), bf16[64,1,64,512]{3,2,1,0:T(8,128)(2,1)}, u32[]{:S(2)}, u32[]{:S(2)}) %all-to-all-start.3) | async-done | bytes 4194336 | tf_op jit(solution)/shard_map/all_to_all | solution.py:101
  534.2 6.9 %reshape.272 = bf16[64,64,4,128]{3,2,1,0:T(4,128)(2,1)} reshape(bf16[64,1,64,512]{3,2,1,0:T(8,128)(2,1)} %all-to-all-done.3) | data formatting | bytes 8388608 | tf_op jit(solution)/shard_map/reshape.6
  547.8 5.1 multiply_convert_fusion.1
  558.2 5.7 all-to-all-start.5
  564.3 5.0 fusion.20
  577.5 82.6 %all-to-all-done.5 = bf16[64,1,64,512]{3,2,1,0:T(8,128)(2,1)} async-done(((bf16[64,1,64,512]{3,2,1,0:T(8,128)(2,1)}), bf16[64,1,64,512]{3,2,1,0:T(8,128)(2,1)}, u32[]{:S(2)}, u32[]{:S(2)}) %all-to-all-start.5) | async-done | bytes 4194336 | tf_op jit(solution)/shard_map/all_to_all | solution.py:117
  660.1 6.7 copy.110
  666.8 5.0 gather_fusion.2
  (104 shorter events, 68.1 us)
Async XLA Ops:
  7.2 140.9 %copy-start = (bf16[1,128,4096]{2,1,0:T(8,128)(2,1)S(1)}, bf16[1,128,4096]{2,1,0:T(8,128)(2,1)}, u32[]{:S(2)}) copy-start(bf16[1,128,4096]{2,1,0:T(8,128)(2,1)} %param.10) | copy-start | bytes 3145732
  7.2 140.9 %all-gather.3.cloned.1.call-start = ((), (), s32[]{:S(2)}) async-start(), calls=%async_computation.7 | async-start | bytes 4259840 | tf_op jit(solution)/shard_map/all_gather | solution.py:39
  8.9 3.7 copy-start.13
  16.2 119.7 %all-to-all-start = ((bf16[64,1,64,512]{3,2,1,0:T(8,128)(2,1)}), bf16[64,1,64,512]{3,2,1,0:T(8,128)(2,1)}, u32[]{:S(2)}, u32[]{:S(2)}) async-start(bf16[64,1,64,512]{3,2,1,0:T(8,128)(2,1)} %bitcast.204), calls=%async_computation | async-start | bytes 8388608 | tf_op jit(solution)/shard_map/all_to_all | solution.py:46
  28.6 166.9 %all-gather.5.cloned.1.call-start = ((), (), s32[]{:S(2)}) async-start(), calls=%async_computation.8 | async-start | bytes 4259840 | tf_op jit(solution)/shard_map/all_gather | solution.py:40
  148.1 3.5 copy-start.7
  152.8 3.2 copy-start.2
  161.7 101.8 %all-to-all-start.1 = ((f32[64,1,256]{2,1,0:T(1,128)}), f32[64,1,256]{2,1,0:T(1,128)S(1)}, u32[]{:S(2)}, u32[]{:S(2)}) async-start(f32[64,1,256]{2,1,0:T(1,128)} %reshape.325), calls=%async_computation.1 | async-start | bytes 131072 | tf_op jit(solution)/shard_map/all_to_all | solution.py:69
  195.4 3.4 copy-start.4
  263.5 7.7 %copy-start.11 = (bf16[512,512]{1,0:T(8,128)(2,1)S(1)}, bf16[512,512]{1,0:T(8,128)(2,1)}, u32[]{:S(2)}) copy-start(bf16[512,512]{1,0:T(8,128)(2,1)} %param.13) | copy-start | bytes 1572868
  263.5 9.1 %copy-start.14 = (s32[8]{0:T(128)S(1)}, s32[8]{0:T(128)}, u32[]{:S(2)}) copy-start(s32[8]{0:T(128)} %param.9) | copy-start | bytes 100
  263.6 103.8 %all-to-all-start.2 = ((bf16[64,2,16384]{2,1,0:T(2,128)(2,1)}), bf16[64,2,16384]{2,1,0:T(2,128)(2,1)}, u32[]{:S(2)}, u32[]{:S(2)}) async-start(bf16[64,2,16384]{2,1,0:T(2,128)(2,1)} %reshape.323), calls=%async_computation.2 | async-start | bytes 8388608 | tf_op jit(solution)/shard_map/all_to_all | solution.py:66
  273.3 120.7 %copy-start.12 = (s32[1024]{0:T(1024)}, s32[1024]{0:T(1024)S(1)}, u32[]{:S(2)}) copy-start(s32[1024]{0:T(1024)S(1)} %pad_clamp_fusion) | copy-start | bytes 12292
  415.6 15.5 %all-to-all-start.4 = ((f32[64,1,256]{2,1,0:T(1,128)}), f32[64,1,256]{2,1,0:T(1,128)S(1)}, u32[]{:S(2)}, u32[]{:S(2)}) async-start(f32[64,1,256]{2,1,0:T(1,128)} %reshape.327), calls=%async_computation.4 | async-start | bytes 131072 | tf_op jit(solution)/shard_map/all_to_all | solution.py:104
  431.1 103.1 %all-to-all-start.3 = ((bf16[64,1,64,512]{3,2,1,0:T(8,128)(2,1)}), bf16[64,1,64,512]{3,2,1,0:T(8,128)(2,1)}, u32[]{:S(2)}, u32[]{:S(2)}) async-start(bf16[64,1,64,512]{3,2,1,0:T(8,128)(2,1)} %bitcast.203), calls=%async_computation.3 | async-start | bytes 8388608 | tf_op jit(solution)/shard_map/all_to_all | solution.py:101
  544.4 3.4 copy-start.3
  552.9 2.0 copy-start.6
  558.2 101.9 %all-to-all-start.5 = ((bf16[64,1,64,512]{3,2,1,0:T(8,128)(2,1)}), bf16[64,1,64,512]{3,2,1,0:T(8,128)(2,1)}, u32[]{:S(2)}, u32[]{:S(2)}) async-start(bf16[64,1,64,512]{3,2,1,0:T(8,128)(2,1)} %bitcast_bitcast_fusion), calls=%async_computation.5 | async-start | bytes 8388608 | tf_op jit(solution)/shard_map/all_to_all | solution.py:117
  563.9 112.7 %reduce-scatter.2.cloned.1.call-start = ((), (), s32[]{:S(2)}) async-start(), calls=%async_computation.9 | async-start | bytes 1310720 | tf_op jit(solution)/shard_map/reduce_scatter | solution.py:132
  564.3 5.0 copy-start.9
  564.3 6.5 copy-start.10
  569.3 2.4 copy-start.5
  571.7 2.2 copy-start.8
  666.8 9.8 %copy-start.1 = (bf16[1,128,4096]{2,1,0:T(8,128)(2,1)S(1)}, bf16[1,128,4096]{2,1,0:T(8,128)(2,1)}, u32[]{:S(2)}) copy-start(bf16[1,128,4096]{2,1,0:T(8,128)(2,1)} %param.10) | copy-start | bytes 3145732
Sparse Core Ops, SparseCore 0:
  10.8 103.1 all-gather.2
  116.7 78.6 all-gather.4
  576.6 25.5 reduce-scatter.1
where the time goes:
time: 694 us; the launch traced here: 683 us
  waiting for transfers between devices  398 us (57%)
  local copies, waits for them, and re-layouts  119 us (17%)
  other arithmetic  79.9 us (12%)
  starting transfers between devices  45.4 us (7%)
  matrix products  26.4 us (4%)
  between operations  14.4 us (2%)
    all_to_all x1, waiting for transfers between devices, local(): lax.all_to_all(send_query, 'dp', split_axis=0, concat_axis=0, tiled=True)  107 us
    all_to_all x1, waiting for transfers between devices, local(): lax.all_to_all(send_grad.astype(jnp.float32), 'dp', split_axis=0, concat_...  95.3 us
    all_to_all x1, waiting for transfers between devices, local(): lax.all_to_all(item_part.astype(jnp.float32), 'dp', split_axis=0, concat_...  88.4 us
    all_to_all x1, waiting for transfers between devices, local(): lax.all_to_all(item_dq, 'dp', split_axis=0, concat_axis=0, tiled=True)  82.6 us
    unnamed x43, local copies, waits for them, and re-layouts  58.6 us
    unnamed x2, other arithmetic  36.5 us
    all_gather x1, waiting for transfers between devices, local(): value_full = lax.all_gather(w_value, 'dp', axis=0, tiled=True)  19.9 us
    convert_element_type x1, local copies, waits for them, and re-layouts, local(): item_part.astype(jnp.float32)  14.6 us
  transfers between devices with their start and end apart: 9, of which 6 were waited for; matrix products, arithmetic and copies ran while one was open for 22% of the time, Pallas kernels for 0%

commit v1 on v0

--- a/solution.py
+++ b/solution.py
@@ -37,7 +37,9 @@
     send_query = send_query.reshape(dp_count, capacity, span_len, local_width)
     flat_states = states.reshape(nbr_dev * nbr_len, dmodel)
     key_full = lax.all_gather(w_key, "dp", axis=0, tiled=True)
-    value_full = lax.all_gather(w_value, "dp", axis=0, tiled=True)
+    value_full = jnp.concatenate(
+        lax.all_to_all(jnp.stack([w_value] * lax.axis_size("dp")), "dp", 0, 0), axis=0
+    )
     key_acc = jnp.dot(flat_states, key_full, preferred_element_type=jnp.float32)
     value_acc = jnp.dot(flat_states, value_full, preferred_element_type=jnp.float32)
     key_rows = key_acc.astype(jnp.bfloat16).reshape(nbr_len, heads_here, HEAD)

time: 694 us -> 745 us (1.073)
  waiting for transfers between devices: 398 us -> 441 us
  starting transfers between devices: 45.4 us -> 53.5 us
    all_to_all x0 -> x1, waiting for transfers between devices: none -> 63.5 us  [local(): lax.all_to_all(jnp.stack([w_value] * lax.axis_size('dp')), 'dp', 0, 0)]
    all_gather x1 -> x0, waiting for transfers between devices: 19.9 us -> none  [local(): value_full = lax.all_gather(w_value, 'dp', axis=0, tiled=True)]
  transfers between devices with their start and end apart: 9 -> 9, of which waited for: 6 -> 6; matrix products, arithmetic and copies ran while one was open for 22% -> 20% of each run, Pallas kernels for 0% -> 0%
where the time goes in v1:
time: 745 us; the launch traced here: 738 us
  waiting for transfers between devices  441 us (59%)
  local copies, waits for them, and re-layouts  121 us (16%)
  other arithmetic  79.9 us (11%)
  starting transfers between devices  53.5 us (7%)
  matrix products  28.5 us (4%)
  between operations  14.7 us (2%)
    all_to_all x1, waiting for transfers between devices, local(): lax.all_to_all(send_query, 'dp', split_axis=0, concat_axis=0, tiled=True)  108 us
    all_to_all x1, waiting for transfers between devices, local(): lax.all_to_all(send_grad.astype(jnp.float32), 'dp', split_axis=0, concat_...  95.3 us
    all_to_all x1, waiting for transfers between devices, local(): lax.all_to_all(item_part.astype(jnp.float32), 'dp', split_axis=0, concat_...  88.4 us
    all_to_all x1, waiting for transfers between devices, local(): lax.all_to_all(item_dq, 'dp', split_axis=0, concat_axis=0, tiled=True)  81.2 us
    all_to_all x1, waiting for transfers between devices, local(): lax.all_to_all(jnp.stack([w_value] * lax.axis_size('dp')), 'dp', 0, 0)  63.5 us
    unnamed x43, local copies, waits for them, and re-layouts  57.7 us
    unnamed x2, other arithmetic  36.5 us
  transfers between devices with their start and end apart: 9, of which 6 were waited for; matrix products, arithmetic and copies ran while one was open for 20% of the time, Pallas kernels for 0%

profile of v1, /device:TPU:4, one launch (start us, length us, event | category | flops | bytes accessed | tf_op | source)
XLA Modules:
  0.0 738.4 jit_solution(7751668628842555635)
XLA Ops:
  15.5 12.5 %all-to-all-start = ((bf16[64,1,64,512]{3,2,1,0:T(8,128)(2,1)}), bf16[64,1,64,512]{3,2,1,0:T(8,128)(2,1)}, u32[]{:S(2)}, u32[]{:S(2)}) async-start(bf16[64,1,64,512]{3,2,1,0:T(8,128)(2,1)} %bitcast.205), calls=%async_computation | async-start | bytes 8388608 | tf_op jit(solution)/shard_map/all_to_all | solution.py:48
  28.7 107.8 %all-to-all-done = bf16[64,1,64,512]{3,2,1,0:T(8,128)(2,1)} async-done(((bf16[64,1,64,512]{3,2,1,0:T(8,128)(2,1)}), bf16[64,1,64,512]{3,2,1,0:T(8,128)(2,1)}, u32[]{:S(2)}, u32[]{:S(2)}) %all-to-all-start) | async-done | bytes 4194336 | tf_op jit(solution)/shard_map/all_to_all | solution.py:48
  139.0 6.0 all-to-all-start.2
  144.9 6.9 reshape.269
  151.9 5.3 copy.81
  165.1 4.8 fusion.2
  170.8 6.9 fusion.4
  177.7 63.5 %all-to-all-done.2 = bf16[64,64,512]{2,1,0:T(8,128)(2,1)} async-done(((bf16[64,64,512]{2,1,0:T(8,128)(2,1)}), bf16[64,64,512]{2,1,0:T(8,128)(2,1)}, u32[]{:S(2)}, u32[]{:S(2)}) %all-to-all-start.2) | async-done | bytes 4194336 | tf_op jit(solution)/shard_map/all_to_all | solution.py:41
  241.2 5.8 all-to-all-start.1
  251.6 4.1 convert_bitcast_fusion
  255.7 14.6 %copy.86 = f32[64,1,64,4,128]{4,3,1,2,0:T(4,128)} copy(f32[64,1,64,4,128]{4,2,0,3,1:T(8,128)} %convert_bitcast_fusion) | data formatting | bytes 16777216 | tf_op jit(solution)/shard_map/convert_element_type | solution.py:69
  270.3 8.0 %convert_bitcast_fusion.1 = bf16[64,64,1,512]{3,2,1,0:T(2,128)(2,1)} fusion(f32[64,1,64,512]{3,1,2,0:T(1,128)} %bitcast.198), kind=kLoop, calls=%fused_computation.76 | loop fusion | flops 2097152 | bytes 12582912
  278.7 28.5 %reduce.4 = bf16[64,64,512]{2,1,0:T(8,128)(2,1)} reduce(bf16[64,64,1,512]{3,2,1,0:T(2,128)(2,1)} %convert_bitcast_fusion.1, bf16[]{:T(256)} %broadcast.140), dimensions={2}, to_apply=%convert_bitcast_fusion.1.reduce_sub_computation | reduce | bytes 8388610
  307.3 7.8 %reshape.329 = bf16[64,2,16384]{2,1,0:T(2,128)(2,1)} reshape(bf16[64,64,512]{2,1,0:T(8,128)(2,1)} %reduce.4) | data formatting | bytes 8388608
  315.1 10.8 %all-to-all-start.3 = ((bf16[64,2,16384]{2,1,0:T(2,128)(2,1)}), bf16[64,2,16384]{2,1,0:T(2,128)(2,1)}, u32[]{:S(2)}, u32[]{:S(2)}) async-start(bf16[64,2,16384]{2,1,0:T(2,128)(2,1)} %reshape.329), calls=%async_computation.3 | async-start | bytes 8388608 | tf_op jit(solution)/shard_map/all_to_all | solution.py:68
  333.7 88.4 %all-to-all-done.3 = bf16[64,2,16384]{2,1,0:T(2,128)(2,1)} async-done(((bf16[64,2,16384]{2,1,0:T(2,128)(2,1)}), bf16[64,2,16384]{2,1,0:T(2,128)(2,1)}, u32[]{:S(2)}, u32[]{:S(2)}) %all-to-all-start.3) | async-done | bytes 4194336 | tf_op jit(solution)/shard_map/all_to_all | solution.py:68
  422.2 19.7 %reshape.330 = bf16[64,64,1,512]{3,2,1,0:T(2,128)(2,1)} reshape(bf16[64,2,16384]{2,1,0:T(2,128)(2,1)} %all-to-all-done.3) | data formatting | bytes 8388608
  441.9 6.9 copy.138
  452.3 5.2 multiply_convert_fusion.2
  460.2 4.8 multiply_reduce_fusion
  470.4 5.5 all-to-all-start.5
  482.1 3.8 all-to-all-done.5
  485.9 6.9 all-to-all-start.4
  493.7 95.3 %all-to-all-done.4 = bf16[64,1,64,512]{3,2,1,0:T(8,128)(2,1)} async-done(((bf16[64,1,64,512]{3,2,1,0:T(8,128)(2,1)}), bf16[64,1,64,512]{3,2,1,0:T(8,128)(2,1)}, u32[]{:S(2)}, u32[]{:S(2)}) %all-to-all-start.4) | async-done | bytes 4194336 | tf_op jit(solution)/shard_map/all_to_all | solution.py:103
  589.0 6.9 reshape.278
  602.6 5.1 multiply_convert_fusion.1
  613.0 5.7 all-to-all-start.6
  619.1 5.0 fusion.20
  627.9 4.7 fusion.5
  633.7 81.2 %all-to-all-done.6 = bf16[64,1,64,512]{3,2,1,0:T(8,128)(2,1)} async-done(((bf16[64,1,64,512]{3,2,1,0:T(8,128)(2,1)}), bf16[64,1,64,512]{3,2,1,0:T(8,128)(2,1)}, u32[]{:S(2)}, u32[]{:S(2)}) %all-to-all-start.6) | async-done | bytes 4194336 | tf_op jit(solution)/shard_map/all_to_all | solution.py:119
  714.9 6.6 copy.110
  721.5 5.0 gather_fusion.2
  (104 shorter events, 73.8 us)
Async XLA Ops:
  7.2 150.0 %copy-start = (bf16[1,128,4096]{2,1,0:T(8,128)(2,1)S(1)}, bf16[1,128,4096]{2,1,0:T(8,128)(2,1)}, u32[]{:S(2)}) copy-start(bf16[1,128,4096]{2,1,0:T(8,128)(2,1)} %param.10) | copy-start | bytes 3145732
  8.3 3.7 copy-start.13
  15.5 121.0 %copy-start.11 = (bf16[64,512]{1,0:T(8,128)(2,1)S(1)}, bf16[64,512]{1,0:T(8,128)(2,1)}, u32[]{:S(2)}) copy-start(bf16[64,512]{1,0:T(8,128)(2,1)} %param.12) | copy-start | bytes 196612
  15.5 121.0 %all-to-all-start = ((bf16[64,1,64,512]{3,2,1,0:T(8,128)(2,1)}), bf16[64,1,64,512]{3,2,1,0:T(8,128)(2,1)}, u32[]{:S(2)}, u32[]{:S(2)}) async-start(bf16[64,1,64,512]{3,2,1,0:T(8,128)(2,1)} %bitcast.205), calls=%async_computation | async-start | bytes 8388608 | tf_op jit(solution)/shard_map/all_to_all | solution.py:48
  28.0 129.2 %all-gather.2.cloned.1.call-start = ((), (), s32[]{:S(2)}) async-start(), calls=%async_computation.8 | async-start | bytes 4259840 | tf_op jit(solution)/shard_map/all_gather | solution.py:39
  139.0 102.2 %all-to-all-start.2 = ((bf16[64,64,512]{2,1,0:T(8,128)(2,1)}), bf16[64,64,512]{2,1,0:T(8,128)(2,1)}, u32[]{:S(2)}, u32[]{:S(2)}) async-start(bf16[64,64,512]{2,1,0:T(8,128)(2,1)} %stack.2), calls=%async_computation.2 | async-start | bytes 8388608 | tf_op jit(solution)/shard_map/all_to_all | solution.py:41
  157.2 3.5 copy-start.7
  161.9 3.2 copy-start.2
  241.2 73.9 %all-to-all-start.1 = ((f32[64,1,256]{2,1,0:T(1,128)}), f32[64,1,256]{2,1,0:T(1,128)S(1)}, u32[]{:S(2)}, u32[]{:S(2)}) async-start(f32[64,1,256]{2,1,0:T(1,128)} %reshape.331), calls=%async_computation.1 | async-start | bytes 131072 | tf_op jit(solution)/shard_map/all_to_all | solution.py:71
  247.0 3.5 copy-start.4
  315.1 10.9 %copy-start.10 = (bf16[512,512]{1,0:T(8,128)(2,1)S(1)}, bf16[512,512]{1,0:T(8,128)(2,1)}, u32[]{:S(2)}) copy-start(bf16[512,512]{1,0:T(8,128)(2,1)} %param.13) | copy-start | bytes 1572868
  315.1 12.3 %copy-start.14 = (s32[8]{0:T(128)S(1)}, s32[8]{0:T(128)}, u32[]{:S(2)}) copy-start(s32[8]{0:T(128)} %param.9) | copy-start | bytes 100
  315.1 107.0 %all-to-all-start.3 = ((bf16[64,2,16384]{2,1,0:T(2,128)(2,1)}), bf16[64,2,16384]{2,1,0:T(2,128)(2,1)}, u32[]{:S(2)}, u32[]{:S(2)}) async-start(bf16[64,2,16384]{2,1,0:T(2,128)(2,1)} %reshape.329), calls=%async_computation.3 | async-start | bytes 8388608 | tf_op jit(solution)/shard_map/all_to_all | solution.py:68
  328.1 120.7 %copy-start.12 = (s32[1024]{0:T(1024)}, s32[1024]{0:T(1024)S(1)}, u32[]{:S(2)}) copy-start(s32[1024]{0:T(1024)S(1)} %pad_clamp_fusion) | copy-start | bytes 12292
  470.4 15.5 %all-to-all-start.5 = ((f32[64,1,256]{2,1,0:T(1,128)}), f32[64,1,256]{2,1,0:T(1,128)S(1)}, u32[]{:S(2)}, u32[]{:S(2)}) async-start(f32[64,1,256]{2,1,0:T(1,128)} %reshape.333), calls=%async_computation.5 | async-start | bytes 131072 | tf_op jit(solution)/shard_map/all_to_all | solution.py:106
  485.9 103.1 %all-to-all-start.4 = ((bf16[64,1,64,512]{3,2,1,0:T(8,128)(2,1)}), bf16[64,1,64,512]{3,2,1,0:T(8,128)(2,1)}, u32[]{:S(2)}, u32[]{:S(2)}) async-start(bf16[64,1,64,512]{3,2,1,0:T(8,128)(2,1)} %bitcast.204), calls=%async_computation.4 | async-start | bytes 8388608 | tf_op jit(solution)/shard_map/all_to_all | solution.py:103
  599.2 3.4 copy-start.3
  607.7 2.0 copy-start.6
  613.0 101.9 %all-to-all-start.6 = ((bf16[64,1,64,512]{3,2,1,0:T(8,128)(2,1)}), bf16[64,1,64,512]{3,2,1,0:T(8,128)(2,1)}, u32[]{:S(2)}, u32[]{:S(2)}) async-start(bf16[64,1,64,512]{3,2,1,0:T(8,128)(2,1)} %bitcast_bitcast_fusion), calls=%async_computation.6 | async-start | bytes 8388608 | tf_op jit(solution)/shard_map/all_to_all | solution.py:119
  618.7 112.7 %reduce-scatter.2.cloned.1.call-start = ((), (), s32[]{:S(2)}) async-start(), calls=%async_computation.9 | async-start | bytes 1310720 | tf_op jit(solution)/shard_map/reduce_scatter | solution.py:134
  619.1 5.0 copy-start.8
  619.1 6.5 copy-start.9
  624.1 2.4 copy-start.5
  721.5 9.8 %copy-start.1 = (bf16[1,128,4096]{2,1,0:T(8,128)(2,1)S(1)}, bf16[1,128,4096]{2,1,0:T(8,128)(2,1)}, u32[]{:S(2)}) copy-start(bf16[1,128,4096]{2,1,0:T(8,128)(2,1)} %param.10) | copy-start | bytes 3145732
Sparse Core Ops, SparseCore 0:
  31.6 96.6 all-gather.1
  632.7 25.5 reduce-scatter.1
